TPU v7x, 32 devices: a whole 2x2x4 slice. The times are simulated.
32 devices in a mesh: expert: 8 (over z, x), dp: 4 (over y, core).
Axes of the slice: x: 2, y: 2, z: 4, core: 2. Of those that a mesh axis runs over, the one named last changes fastest.
Arguments:
- enc_state: bfloat16 [4, 8, 256, 1024], P('dp', 'expert'), may hold values from -6 to 6
- baseline: bfloat16 [4, 8, 256, 1024], P('dp', 'expert'), may hold values from -6 to 6
- enc_keys: bfloat16 [4, 8, 256, 1024], P('dp', 'expert'), may hold values from -4 to 4
- dec_queries: bfloat16 [4, 8, 128, 1024], P('dp', 'expert'), may hold values from -200 to 200
- out_mult: bfloat16 [4, 8, 128, 1024], P('dp', 'expert'), may hold values from -6 to 6
- doc_lengths: int32 [4, 8], P('dp', 'expert'), may hold values from 128 to 256, as said below
- expert_ids: int32 [4, 8, 256], P('dp', 'expert'), may hold values from 0 to 15
- slot_ids: int32 [4, 8, 256], P('dp', 'expert'), may hold values from 0 to 31, as said below
- gate_prob: float32 [4, 8, 256], P('dp', 'expert'), may hold values from 0.2 to 1
- norm_gain: float32 [1024], replicated, may hold values from 0.5 to 2
- w_in: bfloat16 [16, 1024, 2816], P('expert', None, 'dp'), may hold values from -0.1875 to 0.1875
- w_out_t: bfloat16 [16, 1024, 2816], P('expert', None, 'dp'), may hold values from -0.109375 to 0.109375
- w_value: bfloat16 [1024, 1024], replicated, may hold values from -0.1875 to 0.1875
Outputs:
- enc_mult: bfloat16 [4, 8, 256, 1024], P('dp', 'expert')
Inputs may be any that keep to these rules, and one draw needn't show every extreme that they name: `slot_ids`: within one document no two tokens share an expert and a slot, and every token has a slot; one expert has all 32 slots used in every document. `doc_lengths`: some document has all 256 tokens.
All inputs are finite; a program needn't handle non-finite values.
Results may differ from a plain program's by a relative error of at most 0.0069.
Values may be sent and summed in bfloat16 or wider, within the bound.
A program may use at most 128 MiB of HBM per device.

v0:
```python
import functools
import math

import jax
import jax.numpy as jnp
from jax import lax
from jax.experimental import pallas as pl
from jax.experimental.pallas import tpu as pltpu
from jax.sharding import PartitionSpec as P

HEADS = 16
HEAD_DIM = 64


def rescale(pre_act, base_act):
    upper_part = jnp.maximum(jnp.maximum(pre_act, base_act), 0.0)
    lower_part = jnp.maximum(-jnp.minimum(pre_act, base_act), 0.0)
    return upper_part / (upper_part + lower_part + jnp.where(upper_part > 0.0, 0.0, 1.0))


def attend(query_rows, key_rows, mult_rows, length, w_value):
    enc_len = key_rows.shape[0]
    dec_len = query_rows.shape[0]
    queries = query_rows.reshape(dec_len, HEADS, HEAD_DIM)
    keys = key_rows.reshape(enc_len, HEADS, HEAD_DIM)
    mults = mult_rows.reshape(dec_len, HEADS, HEAD_DIM)
    scores = jnp.einsum("qhd,khd->hqk", queries, keys, preferred_element_type=jnp.float32) * (
        1.0 / math.sqrt(HEAD_DIM)
    )
    valid = jnp.arange(enc_len, dtype=jnp.int32) < length
    scores = jnp.where(valid[None, None, :], scores, -jnp.inf)
    top_score = jnp.max(scores, axis=-1, keepdims=True)
    expo = jnp.exp(scores - top_score)
    attn = (expo / jnp.sum(expo, axis=-1, keepdims=True)).astype(jnp.bfloat16)
    value_mult = jnp.einsum("hqk,qhd->khd", attn, mults, preferred_element_type=jnp.float32).astype(
        jnp.bfloat16
    )
    return lax.dot_general(
        value_mult.reshape(enc_len, HEADS * HEAD_DIM),
        w_value,
        (((1,), (1,)), ((), ())),
        preferred_element_type=jnp.float32,
    )


def expert_terms(rows_in, rows_base, rows_mult, part_in, part_out):
    pre_act = jnp.einsum("erd,edf->erf", rows_in, part_in, preferred_element_type=jnp.float32)
    base_act = jnp.einsum("erd,edf->erf", rows_base, part_in, preferred_element_type=jnp.float32)
    hidden_mult = jnp.einsum(
        "erd,edf->erf", rows_mult, part_out, preferred_element_type=jnp.float32
    )
    act_mult = (rescale(pre_act, base_act) * hidden_mult).astype(jnp.bfloat16)
    return jnp.einsum("erf,edf->erd", act_mult, part_in, preferred_element_type=jnp.float32)


def times_t(left, right):
    return lax.dot_general(left, right, (((1,), (1,)), ((), ())), preferred_element_type=jnp.float32)


def whole_kernel(
    n_peers,
    n_dp,
    cap,
    chunk,
    state,
    base_state,
    expert_row,
    place_row,
    gate,
    gain,
    length,
    keys_at,
    queries_at,
    mults_at,
    value_at,
    w_in,
    w_out,
    out,
    keys,
    queries,
    mults,
    value,
    value_mult,
    layer,
    scale,
    sends,
    all_in,
    all_out,
    near_rows,
    far_rows,
    ratio,
    act,
    near_sum,
    far_sum,
    far_got,
    slot_sum,
    back,
    load_sem,
    weight_sem,
    swap_send,
    swap_recv,
    row_send,
    row_recv,
    hop_send,
    hop_recv,
    part_send,
    part_recv,
    back_send,
    back_recv,
):
    n_local = w_in.shape[0]
    tokens, width = state.shape
    rows = n_peers * cap
    n_chunks = width // chunk
    bf16, f32 = jnp.bfloat16, jnp.float32
    me = lax.axis_index("expert")
    dp = lax.axis_index("dp")
    pair = dp + 1 - 2 * lax.rem(dp, 2)
    across = lax.rem(dp + 2, n_dp)
    mesh_id = pl.DeviceIdType.MESH

    loads = []
    for at, (ref, held) in enumerate(
        ((queries_at, queries), (keys_at, keys), (mults_at, mults), (value_at, value))
    ):
        copy = pltpu.make_async_copy(ref, held, load_sem.at[at])
        copy.start()
        loads.append(copy)
    own_weights = []
    for at, (ref, held) in enumerate(((w_in, all_in), (w_out, all_out))):
        copy = pltpu.make_async_copy(ref, held.at[0], weight_sem.at[at])
        copy.start()
        own_weights.append(copy)

    def peer_at(step):
        peer, bit = 0, 1
        while bit < n_peers:
            digit = lax.rem(me // bit, 2)
            peer = peer + bit * (1 - digit if step & bit else digit)
            bit *= 2
        return peer

    barrier = pltpu.get_barrier_semaphore()
    for step in range(1, n_peers):
        pl.semaphore_signal(barrier, inc=1, device_id={"expert": peer_at(step)}, device_id_type=mesh_id)
    for other in (pair, across):
        pl.semaphore_signal(barrier, inc=1, device_id={"dp": other}, device_id_type=mesh_id)

    expert = expert_row[...]
    slot_row = (
        lax.rem(expert, n_local) * rows + lax.div(expert, n_local) * cap + place_row[...]
    )

    def column(row):
        return jnp.transpose(jnp.broadcast_to(row, (128, tokens)))[:, :1]

    def place_rows(a, l, values):
        at = lax.broadcasted_iota(jnp.int32, (rows, tokens), 0) + l * rows
        onehot = jnp.where(at == slot_row, 1.0, 0.0).astype(bf16)
        sends[a, l] = jnp.dot(onehot, values, preferred_element_type=f32).astype(bf16)

    def block_of(src):
        return pl.ds(pl.multiple_of(src * cap, cap), cap)

    def row_copy(a, l, step):
        peer = peer_at(step)
        return pltpu.make_async_remote_copy(
            src_ref=sends.at[a, l, block_of(peer), :],
            dst_ref=near_rows.at[a, l, block_of(me), :],
            send_sem=row_send.at[a, l, step],
            recv_sem=row_recv.at[a, l, step],
            device_id={"expert": peer},
            device_id_type=mesh_id,
        )

    def own_copy(a, l):
        return pltpu.make_async_copy(
            sends.at[a, l, block_of(me), :], near_rows.at[a, l, block_of(me), :], row_recv.at[a, l, 0]
        )

    def send_rows(a, l):
        own_copy(a, l).start()
        for step in range(n_peers - 1, 0, -1):
            row_copy(a, l, step).start()

    def hop_copy(a, l, step):
        src = block_of(peer_at(step))
        return pltpu.make_async_remote_copy(
            src_ref=near_rows.at[a, l, src, :],
            dst_ref=far_rows.at[a, l, src, :],
            send_sem=hop_send.at[a, l, step],
            recv_sem=hop_recv.at[a, l, step],
            device_id={"dp": across},
            device_id_type=mesh_id,
        )

    def relay(a, l, steps):
        for step in steps:
            if step == 0:
                own_copy(a, l).wait()
            else:
                row_copy(a, l, step).wait_recv()
            hop_copy(a, l, step).start()

    def wait_far(a, l):
        for step in range(n_peers):
            hop_copy(a, l, step).wait_recv()

    close = range(0, 2)
    distant = range(2, n_peers)

    token_rows = state[...].astype(f32)
    scale[...] = gain[...] * lax.rsqrt(
        jnp.mean(token_rows * token_rows, axis=-1, keepdims=True) + 1e-06
    )
    inputs = (token_rows * scale[...]).astype(bf16)
    place_rows(0, 0, inputs)
    pl.semaphore_wait(barrier, n_peers + 1)
    send_rows(0, 0)
    base_inputs = (base_state[...].astype(f32) * scale[...]).astype(bf16)
    place_rows(1, 0, base_inputs)
    send_rows(1, 0)
    for l in range(1, n_local):
        place_rows(0, l, inputs)
        send_rows(0, l)
        place_rows(1, l, base_inputs)

    swaps = []
    for at, (ref, held) in enumerate(((w_in, all_in), (w_out, all_out))):
        swap = pltpu.make_async_remote_copy(
            src_ref=ref,
            dst_ref=held.at[1],
            send_sem=swap_send.at[at],
            recv_sem=swap_recv.at[at],
            device_id={"dp": pair},
            device_id_type=mesh_id,
        )
        swap.start()
        swaps.append(swap)

    relay(0, 0, close)
    relay(1, 0, close)
    for l in range(1, n_local):
        relay(0, l, close)

    for copy in loads:
        copy.wait()

    def two_heads(both):
        cols = pl.ds(pl.multiple_of(both * 2 * HEAD_DIM, 2 * HEAD_DIM), 2 * HEAD_DIM)
        query, key, mult = queries[:, cols], keys[:, cols], mults[:, cols]
        first = lax.broadcasted_iota(jnp.int32, query.shape, 1) < HEAD_DIM
        zero = jnp.zeros_like(query)
        found = []
        for head in range(2):
            mine = jnp.where(first, query, zero) if head == 0 else jnp.where(first, zero, query)
            scores = times_t(key, mine) * (1.0 / math.sqrt(HEAD_DIM))
            at = lax.broadcasted_iota(jnp.int32, scores.shape, 0)
            scores = jnp.where(at < length[...], scores, -jnp.inf)
            expo = jnp.exp(scores - jnp.max(scores, axis=0, keepdims=True))
            attn = (expo / jnp.sum(expo, axis=0, keepdims=True)).astype(bf16)
            found.append(jnp.dot(attn, mult, preferred_element_type=f32))
        left = lax.broadcasted_iota(jnp.int32, found[0].shape, 1) < HEAD_DIM
        value_mult[:, cols] = jnp.where(left, found[0], found[1]).astype(bf16)

    pieces = width // (2 * HEAD_DIM)
    bounds = [pieces * at // 4 for at in range(5)]
    for at in range(4):
        pl.loop(bounds[at], bounds[at + 1])(two_heads)
        if at == 1:
            relay(0, 0, distant)

    def chunk_of(c):
        return pl.ds(pl.multiple_of(c * chunk, chunk), chunk)

    @pl.loop(0, n_chunks)
    def _(c):
        layer[:, chunk_of(c)] = times_t(value_mult[...], value[chunk_of(c), :])

    scaled = (column(gate[...]) * layer[...]).astype(bf16)
    for l in range(n_local):
        place_rows(2, l, scaled)
        if l > 0:
            send_rows(1, l)
        send_rows(2, l)
    for l in range(n_local):
        if l > 0:
            relay(1, l, close)
        relay(2, l, close)

    def ratio_of(buf, half, l):
        @pl.loop(0, 2)
        def _(shard):
            weight = all_in[shard, l]
            pre = times_t(buf[0, l], weight)
            base = times_t(buf[1, l], weight)
            ratio[half, l, shard] = rescale(pre, base)

    def acts_of(buf, half, l):
        @pl.loop(0, 2)
        def _(shard):
            hidden = times_t(buf[2, l], all_out[shard, l])
            act[shard] = (ratio[half, l, shard] * hidden).astype(bf16)

    def chunk_sum(l, c):
        cols = chunk_of(c)
        return jnp.dot(act[0], all_in[0, l, :, cols], preferred_element_type=f32) + jnp.dot(
            act[1], all_in[1, l, :, cols], preferred_element_type=f32
        )

    def part_copy(l, c):
        return pltpu.make_async_remote_copy(
            src_ref=far_sum.at[l, :, chunk_of(c)],
            dst_ref=far_got.at[l, :, chunk_of(c)],
            send_sem=part_send.at[l, c],
            recv_sem=part_recv.at[l, c],
            device_id={"dp": across},
            device_id_type=mesh_id,
        )

    def near_part(l):
        acts_of(near_rows, 0, l)

        @pl.loop(0, n_chunks)
        def _(c):
            near_sum[l, :, chunk_of(c)] = chunk_sum(l, c)

    def far_part(l):
        acts_of(far_rows, 1, l)

        @pl.loop(0, n_chunks)
        def _(c):
            far_sum[l, :, chunk_of(c)] = chunk_sum(l, c).astype(bf16)
            part_copy(l, c).start()

    def back_copy(l, c, step):
        peer = peer_at(step)
        return pltpu.make_async_remote_copy(
            src_ref=slot_sum.at[l, block_of(peer), chunk_of(c)],
            dst_ref=back.at[l, block_of(me), chunk_of(c)],
            send_sem=back_send.at[l, c, step],
            recv_sem=back_recv.at[l, c, step],
            device_id={"expert": peer},
            device_id_type=mesh_id,
        )

    def own_back(l, c):
        return pltpu.make_async_copy(
            slot_sum.at[l, block_of(me), chunk_of(c)],
            back.at[l, block_of(me), chunk_of(c)],
            back_recv.at[l, c, 0],
        )

    def send_back(l):
        @pl.loop(0, n_chunks)
        def _(c):
            part_copy(l, c).wait_recv()
            cols = chunk_of(c)
            slot_sum[l, :, cols] = (near_sum[l, :, cols] + far_got[l, :, cols].astype(f32)).astype(bf16)
            for step in range(n_peers - 1, 0, -1):
                back_copy(l, c, step).start()
            own_back(l, c).start()

    last = n_local - 1
    for l in range(n_local):
        if l > 1:
            relay(0, l, distant)
        relay(1, l, distant)
        if l == 0:
            for copy in own_weights:
                copy.wait()
            for swap in swaps:
                swap.wait_recv()
        ratio_of(near_rows, 0, l)
        if l == 0 and n_local > 1:
            relay(0, 1, distant)
        relay(2, l, distant)
        near_part(l)
        wait_far(0, l)
        wait_far(1, l)
        ratio_of(far_rows, 1, l)
        if l > 0:
            send_back(l - 1)
        wait_far(2, l)
        far_part(l)
    send_back(last)

    slot_col = column(slot_row.astype(f32))
    for l in range(n_local):
        at = lax.broadcasted_iota(jnp.int32, (tokens, rows), 1) + l * rows
        pick = jnp.where(at.astype(f32) == slot_col, 1.0, 0.0).astype(bf16)
        for c in range(n_chunks):
            own_back(l, c).wait()
            for step in range(1, n_peers):
                back_copy(l, c, step).wait_recv()
        term = jnp.dot(pick, back[l], preferred_element_type=f32)
        if l == 0:
            near_sum[0] = term
        else:
            near_sum[0] += term
    out[...] = (layer[...] + scale[...] * near_sum[0]).astype(bf16)

    for swap in swaps:
        swap.wait_send()
    for l in range(n_local):
        for a in range(3):
            for step in range(n_peers):
                if step:
                    row_copy(a, l, step).wait_send()
                hop_copy(a, l, step).wait_send()
        for c in range(n_chunks):
            part_copy(l, c).wait_send()
            for step in range(1, n_peers):
                back_copy(l, c, step).wait_send()


def whole_pass(
    state, base_state, keys, queries, mults, length, expert, place, gate, gain, w_in, w_out_t, value, n_peers, n_dp, cap
):
    tokens, width = state.shape
    n_local, _, part = w_in.shape
    w_in, w_out_t = jnp.swapaxes(w_in, 1, 2), jnp.swapaxes(w_out_t, 1, 2)
    rows = n_peers * cap
    chunk = width // 4
    n_chunks = width // chunk
    bf16, f32 = jnp.bfloat16, jnp.float32
    dma = pltpu.SemaphoreType.DMA
    vmem = pl.BlockSpec(memory_space=pltpu.VMEM)
    anyw = pl.BlockSpec(memory_space=pl.ANY)
    wide = (n_local, rows, width)
    return pl.pallas_call(
        functools.partial(whole_kernel, n_peers, n_dp, cap, chunk),
        out_shape=jax.ShapeDtypeStruct((tokens, width), bf16),
        in_specs=[vmem] * 7 + [anyw] * 6,
        out_specs=vmem,
        scratch_shapes=[
            pltpu.VMEM(keys.shape, bf16),
            pltpu.VMEM(queries.shape, bf16),
            pltpu.VMEM(mults.shape, bf16),
            pltpu.VMEM(value.shape, bf16),
            pltpu.VMEM((tokens, width), bf16),
            pltpu.VMEM((tokens, width), f32),
            pltpu.VMEM((tokens, width), f32),
            pltpu.VMEM((3, *wide), bf16),
            pltpu.VMEM((2, n_local, part, width), bf16),
            pltpu.VMEM((2, n_local, part, width), bf16),
            pltpu.VMEM((3, *wide), bf16),
            pltpu.VMEM((3, *wide), bf16),
            pltpu.VMEM((2, n_local, 2, rows, part), f32),
            pltpu.VMEM((2, rows, part), bf16),
            pltpu.VMEM(wide, f32),
            pltpu.VMEM(wide, bf16),
            pltpu.VMEM(wide, bf16),
            pltpu.VMEM(wide, bf16),
            pltpu.VMEM(wide, bf16),
            dma((4,)),
            dma((2,)),
            dma((2,)),
            dma((2,)),
            dma((3, n_local, n_peers)),
            dma((3, n_local, n_peers)),
            dma((3, n_local, n_peers)),
            dma((3, n_local, n_peers)),
            dma((n_local, n_chunks)),
            dma((n_local, n_chunks)),
            dma((n_local, n_chunks, n_peers)),
            dma((n_local, n_chunks, n_peers)),
        ],
        compiler_params=pltpu.CompilerParams(
            collective_id=0, has_side_effects=True, vmem_limit_bytes=60 * 1024 * 1024
        ),
        name="whole_pass",
    )(
        state,
        base_state,
        expert,
        place,
        gate,
        gain[None, :],
        length,
        keys,
        queries,
        mults,
        value,
        w_in,
        w_out_t,
    )


def plain_pass(sent, w_in, w_out_t, n_peers, n_dp):
    near = 2 if n_dp % 2 == 0 else 1
    shards = [(w_in, w_out_t)]
    if near == 2:
        swap = [(i, i ^ 1) for i in range(n_dp)]
        shards.append((lax.ppermute(w_in, "dp", swap), lax.ppermute(w_out_t, "dp", swap)))
    own_rows = tuple(
        lax.all_to_all(a, "expert", split_axis=0, concat_axis=1, tiled=True) for a in sent
    )

    def partial_sum(rows):
        total = expert_terms(*rows, *shards[0])
        for part in shards[1:]:
            total = total + expert_terms(*rows, *part)
        return total

    far = n_dp // near
    far_rows = []
    for hop in range(1, far):
        ahead = [(i, (i + hop * near) % n_dp) for i in range(n_dp)]
        far_rows.append(tuple(lax.ppermute(a, "dp", ahead) for a in own_rows))
    slot_mult = partial_sum(own_rows)
    for hop in range(1, far):
        back = [((i + hop * near) % n_dp, i) for i in range(n_dp)]
        far_part = partial_sum(far_rows[hop - 1]).astype(jnp.bfloat16)
        slot_mult = slot_mult + lax.ppermute(far_part, "dp", back).astype(jnp.float32)

    return lax.all_to_all(
        slot_mult.astype(jnp.bfloat16), "expert", split_axis=1, concat_axis=0, tiled=True
    )


def body(
    enc_state,
    baseline,
    enc_keys,
    dec_queries,
    out_mult,
    doc_lengths,
    expert_ids,
    slot_ids,
    gate_prob,
    norm_gain,
    w_in,
    w_out_t,
    w_value,
):
    enc_len = enc_state.shape[2]
    feature_width = enc_state.shape[3]
    local_experts = w_in.shape[0]
    n_experts = local_experts * lax.axis_size("expert")
    n_dp = lax.axis_size("dp")
    capacity = max(2, 2 * enc_len // n_experts)

    n_peers = lax.axis_size("expert")
    if n_dp == 4 and local_experts == 2 and capacity % 16 == 0 and n_peers & (n_peers - 1) == 0 and feature_width % 512 == 0:
        return whole_pass(
            enc_state[0, 0],
            baseline[0, 0],
            enc_keys[0, 0],
            dec_queries[0, 0],
            out_mult[0, 0],
            doc_lengths,
            expert_ids[0],
            slot_ids[0],
            gate_prob[0],
            norm_gain,
            w_in,
            w_out_t,
            w_value,
            n_peers,
            n_dp,
            capacity,
        )[None, None]

    tokens = enc_state[0, 0].astype(jnp.float32)
    row_scale = norm_gain * lax.rsqrt(jnp.mean(tokens * tokens, axis=-1, keepdims=True) + 1e-06)
    inputs = (tokens * row_scale).astype(jnp.bfloat16)
    base_inputs = (baseline[0, 0].astype(jnp.float32) * row_scale).astype(jnp.bfloat16)
    flat_slot = expert_ids[0, 0] * capacity + slot_ids[0, 0]
    onehot = (
        flat_slot[None, :] == jnp.arange(n_experts * capacity, dtype=jnp.int32)[:, None]
    ).astype(jnp.bfloat16)

    def dispatch(values):
        placed = jnp.dot(onehot, values, preferred_element_type=jnp.float32).astype(jnp.bfloat16)
        return placed.reshape(n_experts, capacity, feature_width)

    layer_mult = attend(
        dec_queries[0, 0], enc_keys[0, 0], out_mult[0, 0], doc_lengths[0, 0], w_value
    )
    scaled_mult = (gate_prob[0, 0][:, None] * layer_mult).astype(jnp.bfloat16)
    sent = (dispatch(inputs), dispatch(base_inputs), dispatch(scaled_mult))
    returned = plain_pass(sent, w_in, w_out_t, n_peers, n_dp)
    per_token = lax.dot_general(
        onehot,
        returned.reshape(n_experts * capacity, feature_width),
        (((0,), (0,)), ((), ())),
        preferred_element_type=jnp.float32,
    )
    result = (layer_mult + row_scale * per_token).astype(jnp.bfloat16)
    return result[None, None]


def solution(mesh):
    in_specs = (
        P("dp", "expert", None, None),
        P("dp", "expert", None, None),
        P("dp", "expert", None, None),
        P("dp", "expert", None, None),
        P("dp", "expert", None, None),
        P("dp", "expert"),
        P("dp", "expert", None),
        P("dp", "expert", None),
        P("dp", "expert", None),
        P(),
        P("expert", None, "dp"),
        P("expert", None, "dp"),
        P(),
    )
    out_specs = P("dp", "expert", None, None)
    return jax.shard_map(body, mesh=mesh, in_specs=in_specs, out_specs=out_specs, check_vma=False)
```

profile of v0, /device:TPU:0, one launch (start us, length us, event | category | flops | bytes accessed | tf_op | source)
XLA Modules:
  0.0 128.5 jit_solution(10506066896986776579)
XLA Ops:
  0.7 125.9 %whole_pass.1 = bf16[256,1024]{1,0:T(8,128)(2,1)} custom-call(bf16[256,1024]{1,0:T(8,128)(2,1)} %bitcast.15, bf16[256,1024]{1,0:T(8,128)(2,1)} %bitcast.16, s32[1,256]{1,0:T(1,128)} %bitcast.21, s32[1,256]{1,0:T(1,128)} %bitcast.22, f32[1,256]{1,0:T(1,128)} %bitcast.23, f32[1,1024]{1,0:T(1,128)} %bitcast.20, s32[1,1]{1,0:T(1,128)S(6)} %copy.15.length, ...), custom_call_target="tpu_custom_call" | custom-call | tf_op jit(solution)/shard_map/whole_pass/pallas_call | solution.py:431
  126.6 1.9 %copy.16 = bf16[1,1,256,1024]{3,2,1,0:T(8,128)(2,1)} copy(bf16[1,1,256,1024]{3,2,1,0:T(8,128)(2,1)} %bitcast.14) | data formatting | bytes 1048576
where the time goes:
time: 129 us; the launch traced here: 128 us
  Pallas kernels  126 us (98%)
  local copies, waits for them, and re-layouts  1.87 us (1%)
    pallas_call x1, Pallas kernels, whole_pass(): pl.pallas_call(functools.partial(whole_kernel, n_peers, n_dp, cap, chunk)...  126 us

commit v1 on v0

v1 whole, which is shorter than its diff:
```python
import functools
import math

import jax
import jax.numpy as jnp
from jax import lax
from jax.experimental import pallas as pl
from jax.experimental.pallas import tpu as pltpu
from jax.sharding import PartitionSpec as P

HEADS = 16
HEAD_DIM = 64


def rescale(pre_act, base_act):
    upper_part = jnp.maximum(jnp.maximum(pre_act, base_act), 0.0)
    lower_part = jnp.maximum(-jnp.minimum(pre_act, base_act), 0.0)
    return upper_part / (upper_part + lower_part + jnp.where(upper_part > 0.0, 0.0, 1.0))


def attend(query_rows, key_rows, mult_rows, length, w_value):
    enc_len = key_rows.shape[0]
    dec_len = query_rows.shape[0]
    queries = query_rows.reshape(dec_len, HEADS, HEAD_DIM)
    keys = key_rows.reshape(enc_len, HEADS, HEAD_DIM)
    mults = mult_rows.reshape(dec_len, HEADS, HEAD_DIM)
    scores = jnp.einsum("qhd,khd->hqk", queries, keys, preferred_element_type=jnp.float32) * (
        1.0 / math.sqrt(HEAD_DIM)
    )
    valid = jnp.arange(enc_len, dtype=jnp.int32) < length
    scores = jnp.where(valid[None, None, :], scores, -jnp.inf)
    top_score = jnp.max(scores, axis=-1, keepdims=True)
    expo = jnp.exp(scores - top_score)
    attn = (expo / jnp.sum(expo, axis=-1, keepdims=True)).astype(jnp.bfloat16)
    value_mult = jnp.einsum("hqk,qhd->khd", attn, mults, preferred_element_type=jnp.float32).astype(
        jnp.bfloat16
    )
    return lax.dot_general(
        value_mult.reshape(enc_len, HEADS * HEAD_DIM),
        w_value,
        (((1,), (1,)), ((), ())),
        preferred_element_type=jnp.float32,
    )


def expert_terms(rows_in, rows_base, rows_mult, part_in, part_out):
    pre_act = jnp.einsum("erd,edf->erf", rows_in, part_in, preferred_element_type=jnp.float32)
    base_act = jnp.einsum("erd,edf->erf", rows_base, part_in, preferred_element_type=jnp.float32)
    hidden_mult = jnp.einsum(
        "erd,edf->erf", rows_mult, part_out, preferred_element_type=jnp.float32
    )
    act_mult = (rescale(pre_act, base_act) * hidden_mult).astype(jnp.bfloat16)
    return jnp.einsum("erf,edf->erd", act_mult, part_in, preferred_element_type=jnp.float32)


def times_t(left, right):
    return lax.dot_general(left, right, (((1,), (1,)), ((), ())), preferred_element_type=jnp.float32)


def whole_kernel(
    n_peers,
    n_dp,
    cap,
    chunk,
    state_at,
    base_at,
    expert_at,
    place_at,
    gate_at,
    gain_at,
    length_at,
    keys_at,
    queries_at,
    mults_at,
    value_at,
    w_in,
    w_out,
    out,
    state,
    base_state,
    expert_row,
    place_row,
    gate,
    gain,
    length,
    keys,
    queries,
    mults,
    value,
    value_mult,
    layer,
    scale,
    sends,
    all_in,
    all_out,
    held,
    ratio,
    act,
    near_sum,
    far_sum,
    far_got,
    slot_sum,
    back,
    load_sem,
    weight_sem,
    swap_send,
    swap_recv,
    row_send,
    row_recv,
    hop_send,
    hop_recv,
    part_send,
    part_recv,
    back_send,
    back_recv,
):
    n_local = w_in.shape[0]
    tokens, width = state.shape
    rows = n_peers * cap
    half = n_peers // 2
    half_rows = half * cap
    n_chunks = width // chunk
    bf16, f32 = jnp.bfloat16, jnp.float32
    me = lax.axis_index("expert")
    dp = lax.axis_index("dp")
    pair = dp + 1 - 2 * lax.rem(dp, 2)
    across = lax.rem(dp + 2, n_dp)
    mesh_id = pl.DeviceIdType.MESH
    my_half = me // half
    inner = lax.rem(my_half + lax.rem(me // (half // 2), 2), 2)

    def peer_at(step):
        peer, bit = 0, 1
        while bit < n_peers:
            digit = lax.rem(me // bit, 2)
            flip = (step // bit) % 2
            peer = peer + bit * (digit + flip - 2 * digit * flip)
            bit *= 2
        return peer

    barrier = pltpu.get_barrier_semaphore()
    for step in range(1, n_peers):
        pl.semaphore_signal(barrier, inc=1, device_id={"expert": peer_at(step)}, device_id_type=mesh_id)
    for other in (pair, across):
        pl.semaphore_signal(barrier, inc=1, device_id={"dp": other}, device_id_type=mesh_id)

    def load(pairs, first_sem):
        copies = []
        for at, (ref, held_at) in enumerate(pairs):
            copy = pltpu.make_async_copy(ref, held_at, load_sem.at[first_sem + at])
            copy.start()
            copies.append(copy)
        return copies

    small = load(
        (
            (state_at, state),
            (gain_at, gain),
            (expert_at, expert_row),
            (place_at, place_row),
            (base_at, base_state),
            (gate_at, gate),
            (length_at, length),
        ),
        0,
    )
    loads = load(((queries_at, queries), (keys_at, keys), (mults_at, mults), (value_at, value)), len(small))
    own_weights = []
    for at, (ref, held_at) in enumerate(((w_in, all_in), (w_out, all_out))):
        copy = pltpu.make_async_copy(ref, held_at.at[0], weight_sem.at[at])
        copy.start()
        own_weights.append(copy)
    for copy in small[:4]:
        copy.wait()

    expert = expert_row[...]
    owner = lax.div(expert, n_local)
    slot_row = lax.rem(expert, n_local) * rows + owner * cap + place_row[...]

    def column(row):
        return jnp.transpose(jnp.broadcast_to(row, (128, tokens)))[:, :1]

    def place_rows(a, l, values):
        at = lax.broadcasted_iota(jnp.int32, (rows, tokens), 0) + l * rows
        onehot = jnp.where(at == slot_row, 1.0, 0.0).astype(bf16)
        sends[a, l] = jnp.dot(onehot, values, preferred_element_type=f32).astype(bf16)

    def block_of(src):
        return pl.ds(pl.multiple_of(src * cap, cap), cap)

    def near_block(src):
        return block_of(lax.rem(src, half))

    def far_block(src):
        return pl.ds(pl.multiple_of(half_rows + lax.rem(src, half) * cap, cap), cap)

    same, cross = 0, 1

    def row_copy(a, l, step):
        peer = peer_at(step)
        kind = step // half
        return pltpu.make_async_remote_copy(
            src_ref=sends.at[a, l, block_of(peer), :],
            dst_ref=held.at[a, l, kind, near_block(me), :],
            send_sem=row_send.at[0],
            recv_sem=row_recv.at[a, l, kind * (step - half + 1)],
            device_id={"expert": peer},
            device_id_type=mesh_id,
        )

    def keep_own(a, l):
        held[a, l, same, near_block(me), :] = sends[a, l, block_of(me), :]

    def hop_copy(a, l, kind, step):
        src = peer_at(step)
        return pltpu.make_async_remote_copy(
            src_ref=held.at[a, l, kind, near_block(src), :],
            dst_ref=held.at[a, l, kind, far_block(src), :],
            send_sem=hop_send.at[0],
            recv_sem=hop_recv.at[a, l, kind],
            device_id={"dp": across},
            device_id_type=mesh_id,
        )

    def own_hop(a, l):
        return pltpu.make_async_remote_copy(
            src_ref=sends.at[a, l, block_of(me), :],
            dst_ref=held.at[a, l, same, far_block(me), :],
            send_sem=hop_send.at[0],
            recv_sem=hop_recv.at[a, l, same],
            device_id={"dp": across},
            device_id_type=mesh_id,
        )

    def await_bytes(ref, sem):
        pltpu.make_async_copy(ref, ref, sem).wait()

    def cross_step(k):
        return n_peers - 1 - lax.rem(k + (half // 2) * inner, half)

    def send_same(a, l):
        for step in range(1, half):
            row_copy(a, l, step).start()

    def send_cross(a, l):
        for step in range(n_peers - 1, half - 1, -1):
            row_copy(a, l, step).start()

    def relay_same(a, l):
        await_bytes(held.at[a, l, same, pl.ds(0, (half - 1) * cap), :], row_recv.at[a, l, 0])
        for step in range(1, half):
            hop_copy(a, l, same, step).start()

    def relay_cross(a, l, ks):
        for k in ks:
            step = cross_step(k)
            await_bytes(held.at[a, l, cross, pl.ds(0, cap), :], row_recv.at[a, l, step - half + 1])
            hop_copy(a, l, cross, step).start()

    first, later = range(0, half // 2), range(half // 2, half)

    def wait_unit(a, l, kind):
        await_bytes(held.at[a, l, kind, pl.ds(half_rows, half_rows), :], hop_recv.at[a, l, kind])

    token_rows = state[...].astype(f32)
    scale[...] = gain[...] * lax.rsqrt(
        jnp.mean(token_rows * token_rows, axis=-1, keepdims=True) + 1e-06
    )
    inputs = (token_rows * scale[...]).astype(bf16)
    for l in range(n_local):
        place_rows(0, l, inputs)
    small[4].wait()
    base_inputs = (base_state[...].astype(f32) * scale[...]).astype(bf16)
    for l in range(n_local):
        place_rows(1, l, base_inputs)
        for a in range(2):
            keep_own(a, l)
    for copy in small[5:]:
        copy.wait()
    with jax.named_scope("barr"):
        pl.semaphore_wait(barrier, n_peers + 1)
    for l in range(n_local):
        for a in range(2):
            own_hop(a, l).start()
    for l in range(n_local):
        for a in range(2):
            send_same(a, l)
        send_cross(l, 0)

    swaps = []
    for at, (ref, held_at) in enumerate(((w_in, all_in), (w_out, all_out))):
        swap = pltpu.make_async_remote_copy(
            src_ref=ref,
            dst_ref=held_at.at[1],
            send_sem=swap_send.at[at],
            recv_sem=swap_recv.at[at],
            device_id={"dp": pair},
            device_id_type=mesh_id,
        )
        swap.start()
        swaps.append(swap)

    for copy in loads:
        copy.wait()

    def two_heads(both):
        cols = pl.ds(pl.multiple_of(both * 2 * HEAD_DIM, 2 * HEAD_DIM), 2 * HEAD_DIM)
        query, key, mult = queries[:, cols], keys[:, cols], mults[:, cols]
        first_head = lax.broadcasted_iota(jnp.int32, query.shape, 1) < HEAD_DIM
        zero = jnp.zeros_like(query)
        found = []
        for head in range(2):
            mine = jnp.where(first_head, query, zero) if head == 0 else jnp.where(first_head, zero, query)
            scores = times_t(key, mine) * (1.0 / math.sqrt(HEAD_DIM))
            at = lax.broadcasted_iota(jnp.int32, scores.shape, 0)
            scores = jnp.where(at < length[...], scores, -jnp.inf)
            expo = jnp.exp(scores - jnp.max(scores, axis=0, keepdims=True))
            attn = (expo / jnp.sum(expo, axis=0, keepdims=True)).astype(bf16)
            found.append(jnp.dot(attn, mult, preferred_element_type=f32))
        left = lax.broadcasted_iota(jnp.int32, found[0].shape, 1) < HEAD_DIM
        value_mult[:, cols] = jnp.where(left, found[0], found[1]).astype(bf16)

    pieces = width // (2 * HEAD_DIM)
    bounds = [pieces * at // 4 for at in range(5)]
    for at in range(4):
        with jax.named_scope(f"attn{at}"):
            pl.loop(bounds[at], bounds[at + 1])(two_heads)
        if at == 2:
            with jax.named_scope("r_s00"):
                relay_same(0, 0)

    def chunk_of(c):
        return pl.ds(pl.multiple_of(c * chunk, chunk), chunk)

    with jax.named_scope("layer"):

        @pl.loop(0, n_chunks)
        def _(c):
            layer[:, chunk_of(c)] = times_t(value_mult[...], value[chunk_of(c), :])

    with jax.named_scope("r_s10"):
        relay_same(1, 0)
    scaled = (column(gate[...]) * layer[...]).astype(bf16)
    for l in range(n_local):
        place_rows(2, l, scaled)
        keep_own(2, l)
        own_hop(2, l).start()
        send_same(2, l)

    def ratio_of(l, kind):
        @pl.loop(0, 2)
        def _(shard):
            weight = all_in[shard, l]
            pre = times_t(held[0, l, kind], weight)
            base = times_t(held[1, l, kind], weight)
            ratio[l, kind, shard] = rescale(pre, base)

    def part_copy(l, kind, c):
        return pltpu.make_async_remote_copy(
            src_ref=far_sum.at[l, kind, :, chunk_of(c)],
            dst_ref=far_got.at[l, kind, :, chunk_of(c)],
            send_sem=part_send.at[0],
            recv_sem=part_recv.at[l, kind, c],
            device_id={"dp": across},
            device_id_type=mesh_id,
        )

    def sums_of(l, kind):
        @pl.loop(0, 2)
        def _(shard):
            hidden = times_t(held[2, l, kind], all_out[shard, l])
            act[shard] = (ratio[l, kind, shard] * hidden).astype(bf16)

        @pl.loop(0, n_chunks)
        def _(c):
            cols = chunk_of(c)
            total = jnp.dot(act[0], all_in[0, l, :, cols], preferred_element_type=f32) + jnp.dot(
                act[1], all_in[1, l, :, cols], preferred_element_type=f32
            )
            near_sum[l, kind, :, cols] = total[:half_rows]
            far_sum[l, kind, :, cols] = total[half_rows:].astype(bf16)
            part_copy(l, kind, c).start()

    def steps_of(kind):
        return range(1, half) if kind == same else range(half, n_peers)

    def back_copy(l, kind, c, step):
        peer = peer_at(step)
        return pltpu.make_async_remote_copy(
            src_ref=slot_sum.at[l, kind, near_block(peer), chunk_of(c)],
            dst_ref=back.at[kind, l, near_block(me), chunk_of(c)],
            send_sem=back_send.at[0],
            recv_sem=back_recv.at[kind, c],
            device_id={"expert": peer},
            device_id_type=mesh_id,
        )

    def send_back(l, kind):
        @pl.loop(0, n_chunks)
        def _(c):
            part_copy(l, kind, c).wait_recv()
            cols = chunk_of(c)
            slot_sum[l, kind, :, cols] = (
                near_sum[l, kind, :, cols] + far_got[l, kind, :, cols].astype(f32)
            ).astype(bf16)
            for step in steps_of(kind)[::-1]:
                back_copy(l, kind, c, step).start()
            if kind == same:
                mine = near_block(me)
                back[same, l, mine, cols] = (
                    near_sum[l, same, mine, cols] + far_got[l, same, mine, cols].astype(f32)
                ).astype(bf16)

    def scoped(name, call, *args):
        with jax.named_scope(name):
            call(*args)

    scoped("r_c00a", relay_cross, 0, 0, first)
    scoped("r_c00b", relay_cross, 0, 0, later)
    send_cross(2, 0)
    scoped("r_s01", relay_same, 0, 1)
    scoped("r_c10a", relay_cross, 1, 0, first)
    scoped("r_c10b", relay_cross, 1, 0, later)
    send_cross(0, 1)
    scoped("r_s11", relay_same, 1, 1)
    with jax.named_scope("weights"):
        for copy in own_weights:
            copy.wait()
        for swap in swaps:
            swap.wait_recv()
    scoped("w_s00", wait_unit, 0, 0, same)
    scoped("w_s10", wait_unit, 1, 0, same)
    scoped("ratio0s", ratio_of, 0, same)
    scoped("r_s20", relay_same, 2, 0)
    scoped("r_c20a", relay_cross, 2, 0, first)
    scoped("r_c20b", relay_cross, 2, 0, later)
    send_cross(1, 1)
    scoped("w_s20", wait_unit, 2, 0, same)
    scoped("sums0s", sums_of, 0, same)
    scoped("r_c01a", relay_cross, 0, 1, first)
    scoped("w_c00", wait_unit, 0, 0, cross)
    scoped("w_c10", wait_unit, 1, 0, cross)
    scoped("ratio0c", ratio_of, 0, cross)
    scoped("r_c01b", relay_cross, 0, 1, later)
    send_cross(2, 1)
    scoped("w_c20", wait_unit, 2, 0, cross)
    scoped("sums0c", sums_of, 0, cross)
    scoped("back0s", send_back, 0, same)
    scoped("r_c11a", relay_cross, 1, 1, first)
    scoped("w_s01", wait_unit, 0, 1, same)
    scoped("w_s11", wait_unit, 1, 1, same)
    scoped("ratio1s", ratio_of, 1, same)
    scoped("r_c11b", relay_cross, 1, 1, later)
    scoped("back0c", send_back, 0, cross)
    scoped("r_c21a", relay_cross, 2, 1, first)
    scoped("w_c01", wait_unit, 0, 1, cross)
    scoped("w_c11", wait_unit, 1, 1, cross)
    scoped("ratio1c", ratio_of, 1, cross)
    scoped("r_c21b", relay_cross, 2, 1, later)
    scoped("r_s21", relay_same, 2, 1)
    scoped("w_c21", wait_unit, 2, 1, cross)
    scoped("sums1c", sums_of, 1, cross)
    scoped("w_s21", wait_unit, 2, 1, same)
    scoped("sums1s", sums_of, 1, same)
    scoped("back1c", send_back, 1, cross)
    scoped("back1s", send_back, 1, same)

    group = owner // half
    other = group + my_half - 2 * group * my_half
    in_half = lax.rem(expert, n_local) * half_rows + lax.rem(owner, half) * cap + place_row[...]
    got_row = other * (n_local * half_rows) + in_half
    got_col = column(got_row.astype(f32))

    def pick_of(kind):
        shape = (tokens, n_local * half_rows)
        at = lax.broadcasted_iota(jnp.int32, shape, 1) + kind * n_local * half_rows
        return jnp.where(at.astype(f32) == got_col, 1.0, 0.0).astype(bf16)

    def wait_back(kind, c):
        remote = len(steps_of(kind)) * cap
        await_bytes(back.at[kind, :, pl.ds(0, remote), chunk_of(c)], back_recv.at[kind, c])

    def got_of(kind, cols):
        return back[kind, :, :, cols].reshape(n_local * half_rows, chunk)

    with jax.named_scope("pick_c"):
        pick = pick_of(cross)
        for c in range(n_chunks):
            wait_back(cross, c)
            cols = chunk_of(c)
            layer[:, cols] += scale[:, cols] * jnp.dot(pick, got_of(cross, cols), preferred_element_type=f32)
    with jax.named_scope("pick_s"):
        pick = pick_of(same)
        for c in range(n_chunks):
            cols = chunk_of(c)
            with jax.named_scope(f"w_{c}"):
                wait_back(same, c)
            out[:, cols] = (
                layer[:, cols] + scale[:, cols] * jnp.dot(pick, got_of(same, cols), preferred_element_type=f32)
            ).astype(bf16)

    with jax.named_scope("drain"):
        for swap in swaps:
            swap.wait_send()
        remote = (n_peers - 1) * cap
        await_bytes(sends.at[:, :, pl.ds(0, remote), :], row_send.at[0])
        await_bytes(sends, hop_send.at[0])
        await_bytes(far_sum, part_send.at[0])
        await_bytes(sends.at[0, :, pl.ds(0, remote), :], back_send.at[0])


def whole_pass(
    state, base_state, keys, queries, mults, length, expert, place, gate, gain, w_in, w_out_t, value, n_peers, n_dp, cap
):
    tokens, width = state.shape
    n_local, _, part = w_in.shape
    w_in, w_out_t = jnp.swapaxes(w_in, 1, 2), jnp.swapaxes(w_out_t, 1, 2)
    rows = n_peers * cap
    half_rows = rows // 2
    chunk = width // 4
    n_chunks = width // chunk
    bf16, f32 = jnp.bfloat16, jnp.float32
    dma = pltpu.SemaphoreType.DMA
    vmem = pl.BlockSpec(memory_space=pltpu.VMEM)
    anyw = pl.BlockSpec(memory_space=pl.ANY)
    halves = (n_local, 2, half_rows, width)
    return pl.pallas_call(
        functools.partial(whole_kernel, n_peers, n_dp, cap, chunk),
        out_shape=jax.ShapeDtypeStruct((tokens, width), bf16),
        in_specs=[anyw] * 13,
        out_specs=vmem,
        scratch_shapes=[
            pltpu.VMEM(state.shape, bf16),
            pltpu.VMEM(base_state.shape, bf16),
            pltpu.VMEM(expert.shape, expert.dtype),
            pltpu.VMEM(place.shape, place.dtype),
            pltpu.VMEM(gate.shape, f32),
            pltpu.VMEM((1, width), f32),
            pltpu.VMEM(length.shape, length.dtype),
            pltpu.VMEM(keys.shape, bf16),
            pltpu.VMEM(queries.shape, bf16),
            pltpu.VMEM(mults.shape, bf16),
            pltpu.VMEM(value.shape, bf16),
            pltpu.VMEM((tokens, width), bf16),
            pltpu.VMEM((tokens, width), f32),
            pltpu.VMEM((tokens, width), f32),
            pltpu.VMEM((3, n_local, rows, width), bf16),
            pltpu.VMEM((2, n_local, part, width), bf16),
            pltpu.VMEM((2, n_local, part, width), bf16),
            pltpu.VMEM((3, n_local, 2, 2 * half_rows, width), bf16),
            pltpu.VMEM((n_local, 2, 2, 2 * half_rows, part), f32),
            pltpu.VMEM((2, 2 * half_rows, part), bf16),
            pltpu.VMEM(halves, f32),
            pltpu.VMEM(halves, bf16),
            pltpu.VMEM(halves, bf16),
            pltpu.VMEM(halves, bf16),
            pltpu.VMEM((2, n_local, half_rows, width), bf16),
            dma((11,)),
            dma((2,)),
            dma((2,)),
            dma((2,)),
            dma((1,)),
            dma((3, n_local, 1 + n_peers // 2)),
            dma((1,)),
            dma((3, n_local, 2)),
            dma((1,)),
            dma((n_local, 2, n_chunks)),
            dma((1,)),
            dma((2, n_chunks)),
        ],
        compiler_params=pltpu.CompilerParams(
            collective_id=0, has_side_effects=True, vmem_limit_bytes=60 * 1024 * 1024
        ),
        name="whole_pass",
    )(
        state,
        base_state,
        expert,
        place,
        gate,
        gain[None, :],
        length,
        keys,
        queries,
        mults,
        value,
        w_in,
        w_out_t,
    )


def plain_pass(sent, w_in, w_out_t, n_peers, n_dp):
    near = 2 if n_dp % 2 == 0 else 1
    shards = [(w_in, w_out_t)]
    if near == 2:
        swap = [(i, i ^ 1) for i in range(n_dp)]
        shards.append((lax.ppermute(w_in, "dp", swap), lax.ppermute(w_out_t, "dp", swap)))
    own_rows = tuple(
        lax.all_to_all(a, "expert", split_axis=0, concat_axis=1, tiled=True) for a in sent
    )

    def partial_sum(rows):
        total = expert_terms(*rows, *shards[0])
        for part in shards[1:]:
            total = total + expert_terms(*rows, *part)
        return total

    far = n_dp // near
    far_rows = []
    for hop in range(1, far):
        ahead = [(i, (i + hop * near) % n_dp) for i in range(n_dp)]
        far_rows.append(tuple(lax.ppermute(a, "dp", ahead) for a in own_rows))
    slot_mult = partial_sum(own_rows)
    for hop in range(1, far):
        back = [((i + hop * near) % n_dp, i) for i in range(n_dp)]
        far_part = partial_sum(far_rows[hop - 1]).astype(jnp.bfloat16)
        slot_mult = slot_mult + lax.ppermute(far_part, "dp", back).astype(jnp.float32)

    return lax.all_to_all(
        slot_mult.astype(jnp.bfloat16), "expert", split_axis=1, concat_axis=0, tiled=True
    )


def body(
    enc_state,
    baseline,
    enc_keys,
    dec_queries,
    out_mult,
    doc_lengths,
    expert_ids,
    slot_ids,
    gate_prob,
    norm_gain,
    w_in,
    w_out_t,
    w_value,
):
    enc_len = enc_state.shape[2]
    feature_width = enc_state.shape[3]
    local_experts = w_in.shape[0]
    n_experts = local_experts * lax.axis_size("expert")
    n_dp = lax.axis_size("dp")
    capacity = max(2, 2 * enc_len // n_experts)

    n_peers = lax.axis_size("expert")
    if n_dp == 4 and local_experts == 2 and capacity % 16 == 0 and n_peers >= 4 and n_peers & (n_peers - 1) == 0 and feature_width % 512 == 0:
        return whole_pass(
            enc_state[0, 0],
            baseline[0, 0],
            enc_keys[0, 0],
            dec_queries[0, 0],
            out_mult[0, 0],
            doc_lengths,
            expert_ids[0],
            slot_ids[0],
            gate_prob[0],
            norm_gain,
            w_in,
            w_out_t,
            w_value,
            n_peers,
            n_dp,
            capacity,
        )[None, None]

    tokens = enc_state[0, 0].astype(jnp.float32)
    row_scale = norm_gain * lax.rsqrt(jnp.mean(tokens * tokens, axis=-1, keepdims=True) + 1e-06)
    inputs = (tokens * row_scale).astype(jnp.bfloat16)
    base_inputs = (baseline[0, 0].astype(jnp.float32) * row_scale).astype(jnp.bfloat16)
    flat_slot = expert_ids[0, 0] * capacity + slot_ids[0, 0]
    onehot = (
        flat_slot[None, :] == jnp.arange(n_experts * capacity, dtype=jnp.int32)[:, None]
    ).astype(jnp.bfloat16)

    def dispatch(values):
        placed = jnp.dot(onehot, values, preferred_element_type=jnp.float32).astype(jnp.bfloat16)
        return placed.reshape(n_experts, capacity, feature_width)

    layer_mult = attend(
        dec_queries[0, 0], enc_keys[0, 0], out_mult[0, 0], doc_lengths[0, 0], w_value
    )
    scaled_mult = (gate_prob[0, 0][:, None] * layer_mult).astype(jnp.bfloat16)
    sent = (dispatch(inputs), dispatch(base_inputs), dispatch(scaled_mult))
    returned = plain_pass(sent, w_in, w_out_t, n_peers, n_dp)
    per_token = lax.dot_general(
        onehot,
        returned.reshape(n_experts * capacity, feature_width),
        (((0,), (0,)), ((), ())),
        preferred_element_type=jnp.float32,
    )
    result = (layer_mult + row_scale * per_token).astype(jnp.bfloat16)
    return result[None, None]


def solution(mesh):
    in_specs = (
        P("dp", "expert", None, None),
        P("dp", "expert", None, None),
        P("dp", "expert", None, None),
        P("dp", "expert", None, None),
        P("dp", "expert", None, None),
        P("dp", "expert"),
        P("dp", "expert", None),
        P("dp", "expert", None),
        P("dp", "expert", None),
        P(),
        P("expert", None, "dp"),
        P("expert", None, "dp"),
        P(),
    )
    out_specs = P("dp", "expert", None, None)
    return jax.shard_map(body, mesh=mesh, in_specs=in_specs, out_specs=out_specs, check_vma=False)
```

time: 129 us -> 109 us (0.84)
  Pallas kernels: 126 us -> 106 us
    pallas_call x1, Pallas kernels: 126 us -> 106 us  [whole_pass(): pl.pallas_call(functools.partial(whole_kernel, n_peers, n_dp, cap, chunk)...]
where the time goes in v1:
time: 109 us
  Pallas kernels  106 us (97%)
  local copies, waits for them, and re-layouts  1.87 us (2%)
    pallas_call x1, Pallas kernels, whole_pass(): pl.pallas_call(functools.partial(whole_kernel, n_peers, n_dp, cap, chunk)...  106 us

profile of v1, /device:TPU:0, one launch (start us, length us, event | category | flops | bytes accessed | tf_op | source)
XLA Modules:
  0.0 108.5 jit_solution(5666877499767857343)
XLA Ops:
  0.7 106.0 %whole_pass.1 = bf16[256,1024]{1,0:T(8,128)(2,1)} custom-call(bf16[256,1024]{1,0:T(8,128)(2,1)} %bitcast.15, bf16[256,1024]{1,0:T(8,128)(2,1)} %bitcast.16, s32[1,256]{1,0:T(1,128)} %bitcast.21, s32[1,256]{1,0:T(1,128)} %bitcast.22, f32[1,256]{1,0:T(1,128)} %bitcast.23, f32[1,1024]{1,0:T(1,128)} %bitcast.20, s32[1,1]{1,0:T(1,128)S(6)} %copy.15.length_at, ...), custom_call_target="tpu_custom_call" | custom-call | tf_op jit(solution)/shard_map/whole_pass/pallas_call | solution.py:527
  106.7 1.9 %copy.16 = bf16[1,1,256,1024]{3,2,1,0:T(8,128)(2,1)} copy(bf16[1,1,256,1024]{3,2,1,0:T(8,128)(2,1)} %bitcast.14) | data formatting | bytes 1048576

commit v2 on v1

--- a/solution.py
+++ b/solution.py
@@ -203,7 +203,7 @@
             src_ref=sends.at[a, l, block_of(peer), :],
             dst_ref=held.at[a, l, kind, near_block(me), :],
             send_sem=row_send.at[0],
-            recv_sem=row_recv.at[a, l, kind * (step - half + 1)],
+            recv_sem=row_recv.at[a, l, step],
             device_id={"expert": peer},
             device_id_type=mesh_id,
         )
@@ -235,29 +235,25 @@
     def await_bytes(ref, sem):
         pltpu.make_async_copy(ref, ref, sem).wait()
 
-    def cross_step(k):
-        return n_peers - 1 - lax.rem(k + (half // 2) * inner, half)
+    cross_steps = [*range(n_peers - 2, half - 1, -2), *range(n_peers - 1, half, -2)]
+    first, later = cross_steps[: half // 2], cross_steps[half // 2 :]
 
     def send_same(a, l):
         for step in range(1, half):
             row_copy(a, l, step).start()
 
     def send_cross(a, l):
-        for step in range(n_peers - 1, half - 1, -1):
+        for step in cross_steps:
             row_copy(a, l, step).start()
 
+    def relay(a, l, steps):
+        for step in steps:
+            kind = step // half
+            await_bytes(held.at[a, l, kind, pl.ds(0, cap), :], row_recv.at[a, l, step])
+            hop_copy(a, l, kind, step).start()
+
     def relay_same(a, l):
-        await_bytes(held.at[a, l, same, pl.ds(0, (half - 1) * cap), :], row_recv.at[a, l, 0])
-        for step in range(1, half):
-            hop_copy(a, l, same, step).start()
-
-    def relay_cross(a, l, ks):
-        for k in ks:
-            step = cross_step(k)
-            await_bytes(held.at[a, l, cross, pl.ds(0, cap), :], row_recv.at[a, l, step - half + 1])
-            hop_copy(a, l, cross, step).start()
-
-    first, later = range(0, half // 2), range(half // 2, half)
+        relay(a, l, range(1, half))
 
     def wait_unit(a, l, kind):
         await_bytes(held.at[a, l, kind, pl.ds(half_rows, half_rows), :], hop_recv.at[a, l, kind])
@@ -282,10 +278,12 @@
     for l in range(n_local):
         for a in range(2):
             own_hop(a, l).start()
-    for l in range(n_local):
-        for a in range(2):
-            send_same(a, l)
-        send_cross(l, 0)
+    send_same(0, 0)
+    send_cross(0, 0)
+    send_same(1, 0)
+    send_same(0, 1)
+    send_cross(1, 0)
+    send_same(1, 1)
 
     swaps = []
     for at, (ref, held_at) in enumerate(((w_in, all_in), (w_out, all_out))):
@@ -325,9 +323,10 @@
     for at in range(4):
         with jax.named_scope(f"attn{at}"):
             pl.loop(bounds[at], bounds[at + 1])(two_heads)
-        if at == 2:
-            with jax.named_scope("r_s00"):
-                relay_same(0, 0)
+    with jax.named_scope("r_s00"):
+        relay(0, 0, range(1, half - 1))
+    with jax.named_scope("r_c00a"):
+        relay(0, 0, first[:1])
 
     def chunk_of(c):
         return pl.ds(pl.multiple_of(c * chunk, chunk), chunk)
@@ -338,8 +337,8 @@
         def _(c):
             layer[:, chunk_of(c)] = times_t(value_mult[...], value[chunk_of(c), :])
 
-    with jax.named_scope("r_s10"):
-        relay_same(1, 0)
+    with jax.named_scope("r_s00b"):
+        relay(0, 0, [half - 1])
     scaled = (column(gate[...]) * layer[...]).astype(bf16)
     for l in range(n_local):
         place_rows(2, l, scaled)
@@ -365,7 +364,7 @@
             device_id_type=mesh_id,
         )
 
-    def sums_of(l, kind):
+    def sums_of(l, kind, then=None):
         @pl.loop(0, 2)
         def _(shard):
             hidden = times_t(held[2, l, kind], all_out[shard, l])
@@ -380,6 +379,8 @@
             near_sum[l, kind, :, cols] = total[:half_rows]
             far_sum[l, kind, :, cols] = total[half_rows:].astype(bf16)
             part_copy(l, kind, c).start()
+            if then is not None:
+                then(c)
 
     def steps_of(kind):
         return range(1, half) if kind == same else range(half, n_peers)
@@ -395,34 +396,32 @@
             device_id_type=mesh_id,
         )
 
+    def back_chunk(l, kind, c):
+        part_copy(l, kind, c).wait_recv()
+        cols = chunk_of(c)
+        slot_sum[l, kind, :, cols] = (
+            near_sum[l, kind, :, cols] + far_got[l, kind, :, cols].astype(f32)
+        ).astype(bf16)
+        for step in steps_of(kind)[::-1]:
+            back_copy(l, kind, c, step).start()
+        if kind == same:
+            mine = near_block(me)
+            back[same, l, mine, cols] = (
+                near_sum[l, same, mine, cols] + far_got[l, same, mine, cols].astype(f32)
+            ).astype(bf16)
+
     def send_back(l, kind):
-        @pl.loop(0, n_chunks)
-        def _(c):
-            part_copy(l, kind, c).wait_recv()
-            cols = chunk_of(c)
-            slot_sum[l, kind, :, cols] = (
-                near_sum[l, kind, :, cols] + far_got[l, kind, :, cols].astype(f32)
-            ).astype(bf16)
-            for step in steps_of(kind)[::-1]:
-                back_copy(l, kind, c, step).start()
-            if kind == same:
-                mine = near_block(me)
-                back[same, l, mine, cols] = (
-                    near_sum[l, same, mine, cols] + far_got[l, same, mine, cols].astype(f32)
-                ).astype(bf16)
+        pl.loop(0, n_chunks)(functools.partial(back_chunk, l, kind))
 
     def scoped(name, call, *args):
         with jax.named_scope(name):
             call(*args)
 
-    scoped("r_c00a", relay_cross, 0, 0, first)
-    scoped("r_c00b", relay_cross, 0, 0, later)
+    scoped("r_c00b", relay, 0, 0, first[1:])
+    scoped("r_c00c", relay, 0, 0, later)
     send_cross(2, 0)
+    scoped("r_s10", relay_same, 1, 0)
     scoped("r_s01", relay_same, 0, 1)
-    scoped("r_c10a", relay_cross, 1, 0, first)
-    scoped("r_c10b", relay_cross, 1, 0, later)
-    send_cross(0, 1)
-    scoped("r_s11", relay_same, 1, 1)
     with jax.named_scope("weights"):
         for copy in own_weights:
             copy.wait()
@@ -431,38 +430,41 @@
     scoped("w_s00", wait_unit, 0, 0, same)
     scoped("w_s10", wait_unit, 1, 0, same)
     scoped("ratio0s", ratio_of, 0, same)
+    scoped("r_c10a", relay, 1, 0, first)
+    scoped("r_c10b", relay, 1, 0, later)
+    send_cross(0, 1)
+    scoped("r_s11", relay_same, 1, 1)
     scoped("r_s20", relay_same, 2, 0)
-    scoped("r_c20a", relay_cross, 2, 0, first)
-    scoped("r_c20b", relay_cross, 2, 0, later)
+    scoped("r_c20a", relay, 2, 0, first)
+    scoped("r_c20b", relay, 2, 0, later)
     send_cross(1, 1)
     scoped("w_s20", wait_unit, 2, 0, same)
     scoped("sums0s", sums_of, 0, same)
-    scoped("r_c01a", relay_cross, 0, 1, first)
+    scoped("r_c01a", relay, 0, 1, first)
     scoped("w_c00", wait_unit, 0, 0, cross)
     scoped("w_c10", wait_unit, 1, 0, cross)
     scoped("ratio0c", ratio_of, 0, cross)
-    scoped("r_c01b", relay_cross, 0, 1, later)
+    scoped("r_c01b", relay, 0, 1, later)
     send_cross(2, 1)
     scoped("w_c20", wait_unit, 2, 0, cross)
     scoped("sums0c", sums_of, 0, cross)
-    scoped("back0s", send_back, 0, same)
-    scoped("r_c11a", relay_cross, 1, 1, first)
     scoped("w_s01", wait_unit, 0, 1, same)
     scoped("w_s11", wait_unit, 1, 1, same)
     scoped("ratio1s", ratio_of, 1, same)
-    scoped("r_c11b", relay_cross, 1, 1, later)
+    scoped("r_c11a", relay, 1, 1, first)
+    scoped("r_c11b", relay, 1, 1, later)
+    scoped("back0s", send_back, 0, same)
+    scoped("r_c21a", relay, 2, 1, first)
     scoped("back0c", send_back, 0, cross)
-    scoped("r_c21a", relay_cross, 2, 1, first)
     scoped("w_c01", wait_unit, 0, 1, cross)
     scoped("w_c11", wait_unit, 1, 1, cross)
     scoped("ratio1c", ratio_of, 1, cross)
-    scoped("r_c21b", relay_cross, 2, 1, later)
+    scoped("r_c21b", relay, 2, 1, later)
     scoped("r_s21", relay_same, 2, 1)
     scoped("w_c21", wait_unit, 2, 1, cross)
     scoped("sums1c", sums_of, 1, cross)
     scoped("w_s21", wait_unit, 2, 1, same)
-    scoped("sums1s", sums_of, 1, same)
-    scoped("back1c", send_back, 1, cross)
+    scoped("sums1s", sums_of, 1, same, functools.partial(back_chunk, 1, cross))
     scoped("back1s", send_back, 1, same)
 
     group = owner // half
@@ -526,7 +528,7 @@
     halves = (n_local, 2, half_rows, width)
     return pl.pallas_call(
         functools.partial(whole_kernel, n_peers, n_dp, cap, chunk),
-        out_shape=jax.ShapeDtypeStruct((tokens, width), bf16),
+        out_shape=pltpu.VMEM((tokens, width), bf16),
         in_specs=[anyw] * 13,
         out_specs=vmem,
         scratch_shapes=[
@@ -560,7 +562,7 @@
             dma((2,)),
             dma((2,)),
             dma((1,)),
-            dma((3, n_local, 1 + n_peers // 2)),
+            dma((3, n_local, n_peers)),
             dma((1,)),
             dma((3, n_local, 2)),
             dma((1,)),

time: 109 us -> 105 us (0.963)
  Pallas kernels: 106 us -> 103 us
    pallas_call x1, Pallas kernels: 106 us -> 103 us  [whole_pass(): pl.pallas_call(functools.partial(whole_kernel, n_peers, n_dp, cap, chunk)...]
where the time goes in v2:
time: 105 us; the launch traced here: 104 us
  Pallas kernels  103 us (98%)
    pallas_call x1, Pallas kernels, whole_pass(): pl.pallas_call(functools.partial(whole_kernel, n_peers, n_dp, cap, chunk)...  103 us

profile of v2, /device:TPU:0, one launch (start us, length us, event | category | flops | bytes accessed | tf_op | source)
XLA Modules:
  0.0 104.4 jit_solution(17681364544571107221)
XLA Ops:
  0.7 103.0 %whole_pass.1 = bf16[256,1024]{1,0:T(8,128)(2,1)S(1)} custom-call(bf16[256,1024]{1,0:T(8,128)(2,1)} %bitcast.15, bf16[256,1024]{1,0:T(8,128)(2,1)} %bitcast.16, s32[1,256]{1,0:T(1,128)} %bitcast.21, s32[1,256]{1,0:T(1,128)} %bitcast.22, f32[1,256]{1,0:T(1,128)} %bitcast.23, f32[1,1024]{1,0:T(1,128)} %bitcast.20, s32[1,1]{1,0:T(1,128)S(6)} %copy.16.length_at, ...), custom_call_target="tpu_custom_call" | custom-call | tf_op jit(solution)/shard_map/whole_pass/pallas_call | solution.py:529
  103.6 0.8 copy.15

commit v3 on v2

--- a/solution.py
+++ b/solution.py
@@ -196,6 +196,13 @@
 
     same, cross = 0, 1
 
+    def arrival_of(a, l, step):
+        at = a + 3 * l
+        if step >= half:
+            return at * half + step - half
+        apart = 3 * n_local * half
+        return apart + at if at or step == 1 else apart + 3 * n_local + step - 2
+
     def row_copy(a, l, step):
         peer = peer_at(step)
         kind = step // half
@@ -203,7 +210,7 @@
             src_ref=sends.at[a, l, block_of(peer), :],
             dst_ref=held.at[a, l, kind, near_block(me), :],
             send_sem=row_send.at[0],
-            recv_sem=row_recv.at[a, l, step],
+            recv_sem=row_recv.at[arrival_of(a, l, step)],
             device_id={"expert": peer},
             device_id_type=mesh_id,
         )
@@ -246,14 +253,27 @@
         for step in cross_steps:
             row_copy(a, l, step).start()
 
+    order = [(a, l) for l in range(n_local) for a in range(3)]
+
+    def next_cross(at):
+        for ahead, mine in ((1, 0), (2, 1)):
+            if at + ahead < len(order):
+
+                @pl.when(inner == mine)
+                def _():
+                    send_cross(*order[at + ahead])
+
+    def relay_same(a, l, steps=range(1, half)):
+        if 1 in steps:
+            await_bytes(held.at[a, l, same, pl.ds(0, (half - 1) * cap), :], row_recv.at[arrival_of(a, l, 1)])
+        for step in steps:
+            hop_copy(a, l, same, step).start()
+
     def relay(a, l, steps):
         for step in steps:
             kind = step // half
-            await_bytes(held.at[a, l, kind, pl.ds(0, cap), :], row_recv.at[a, l, step])
+            await_bytes(held.at[a, l, kind, pl.ds(0, cap), :], row_recv.at[arrival_of(a, l, step)])
             hop_copy(a, l, kind, step).start()
-
-    def relay_same(a, l):
-        relay(a, l, range(1, half))
 
     def wait_unit(a, l, kind):
         await_bytes(held.at[a, l, kind, pl.ds(half_rows, half_rows), :], hop_recv.at[a, l, kind])
@@ -263,27 +283,33 @@
         jnp.mean(token_rows * token_rows, axis=-1, keepdims=True) + 1e-06
     )
     inputs = (token_rows * scale[...]).astype(bf16)
-    for l in range(n_local):
-        place_rows(0, l, inputs)
+    place_rows(0, 0, inputs)
+    with jax.named_scope("barr"):
+        pl.semaphore_wait(barrier, n_peers + 1)
+    own_hop(0, 0).start()
+    send_same(0, 0)
+    send_cross(0, 0)
     small[4].wait()
     base_inputs = (base_state[...].astype(f32) * scale[...]).astype(bf16)
+    place_rows(1, 0, base_inputs)
+    own_hop(1, 0).start()
+    send_same(1, 0)
+    place_rows(0, 1, inputs)
+    own_hop(0, 1).start()
+    send_same(0, 1)
+
+    @pl.when(inner == 1)
+    def _():
+        send_cross(1, 0)
+
+    place_rows(1, 1, base_inputs)
+    own_hop(1, 1).start()
+    send_same(1, 1)
     for l in range(n_local):
-        place_rows(1, l, base_inputs)
         for a in range(2):
             keep_own(a, l)
     for copy in small[5:]:
         copy.wait()
-    with jax.named_scope("barr"):
-        pl.semaphore_wait(barrier, n_peers + 1)
-    for l in range(n_local):
-        for a in range(2):
-            own_hop(a, l).start()
-    send_same(0, 0)
-    send_cross(0, 0)
-    send_same(1, 0)
-    send_same(0, 1)
-    send_cross(1, 0)
-    send_same(1, 1)
 
     swaps = []
     for at, (ref, held_at) in enumerate(((w_in, all_in), (w_out, all_out))):
@@ -319,14 +345,12 @@
         value_mult[:, cols] = jnp.where(left, found[0], found[1]).astype(bf16)
 
     pieces = width // (2 * HEAD_DIM)
-    bounds = [pieces * at // 4 for at in range(5)]
-    for at in range(4):
-        with jax.named_scope(f"attn{at}"):
-            pl.loop(bounds[at], bounds[at + 1])(two_heads)
+    with jax.named_scope("attn0"):
+        pl.loop(0, pieces - 1)(two_heads)
     with jax.named_scope("r_s00"):
         relay(0, 0, range(1, half - 1))
-    with jax.named_scope("r_c00a"):
-        relay(0, 0, first[:1])
+    with jax.named_scope("attn1"):
+        pl.loop(pieces - 1, pieces)(two_heads)
 
     def chunk_of(c):
         return pl.ds(pl.multiple_of(c * chunk, chunk), chunk)
@@ -337,6 +361,8 @@
         def _(c):
             layer[:, chunk_of(c)] = times_t(value_mult[...], value[chunk_of(c), :])
 
+    with jax.named_scope("r_c00a"):
+        relay(0, 0, first[:1])
     with jax.named_scope("r_s00b"):
         relay(0, 0, [half - 1])
     scaled = (column(gate[...]) * layer[...]).astype(bf16)
@@ -354,24 +380,25 @@
             base = times_t(held[1, l, kind], weight)
             ratio[l, kind, shard] = rescale(pre, base)
 
+    last = n_local - 1
+
     def part_copy(l, kind, c):
         return pltpu.make_async_remote_copy(
             src_ref=far_sum.at[l, kind, :, chunk_of(c)],
             dst_ref=far_got.at[l, kind, :, chunk_of(c)],
             send_sem=part_send.at[0],
-            recv_sem=part_recv.at[l, kind, c],
+            recv_sem=part_recv.at[kind if l < last else 2 + kind * n_chunks + c],
             device_id={"dp": across},
             device_id_type=mesh_id,
         )
 
-    def sums_of(l, kind, then=None):
+    def sums_of(l, kind, then=None, once=None):
         @pl.loop(0, 2)
         def _(shard):
             hidden = times_t(held[2, l, kind], all_out[shard, l])
             act[shard] = (ratio[l, kind, shard] * hidden).astype(bf16)
 
-        @pl.loop(0, n_chunks)
-        def _(c):
+        def sum_chunk(c):
             cols = chunk_of(c)
             total = jnp.dot(act[0], all_in[0, l, :, cols], preferred_element_type=f32) + jnp.dot(
                 act[1], all_in[1, l, :, cols], preferred_element_type=f32
@@ -379,8 +406,20 @@
             near_sum[l, kind, :, cols] = total[:half_rows]
             far_sum[l, kind, :, cols] = total[half_rows:].astype(bf16)
             part_copy(l, kind, c).start()
-            if then is not None:
+
+        if once is not None:
+            sum_chunk(0)
+            once()
+        if then is None:
+            pl.loop(0 if once is None else 1, n_chunks)(sum_chunk)
+        else:
+
+            @pl.loop(1, n_chunks)
+            def _(c):
+                sum_chunk(c - 1)
                 then(c)
+
+            sum_chunk(n_chunks - 1)
 
     def steps_of(kind):
         return range(1, half) if kind == same else range(half, n_peers)
@@ -397,7 +436,8 @@
         )
 
     def back_chunk(l, kind, c):
-        part_copy(l, kind, c).wait_recv()
+        if l == last:
+            part_copy(l, kind, c).wait_recv()
         cols = chunk_of(c)
         slot_sum[l, kind, :, cols] = (
             near_sum[l, kind, :, cols] + far_got[l, kind, :, cols].astype(f32)
@@ -410,8 +450,10 @@
                 near_sum[l, same, mine, cols] + far_got[l, same, mine, cols].astype(f32)
             ).astype(bf16)
 
-    def send_back(l, kind):
-        pl.loop(0, n_chunks)(functools.partial(back_chunk, l, kind))
+    def send_back(l, kind, begin=0, end=n_chunks):
+        if l < last and begin == 0:
+            await_bytes(far_got.at[l, kind], part_recv.at[kind])
+        pl.loop(begin, end)(functools.partial(back_chunk, l, kind))
 
     def scoped(name, call, *args):
         with jax.named_scope(name):
@@ -419,9 +461,10 @@
 
     scoped("r_c00b", relay, 0, 0, first[1:])
     scoped("r_c00c", relay, 0, 0, later)
-    send_cross(2, 0)
+    next_cross(0)
     scoped("r_s10", relay_same, 1, 0)
     scoped("r_s01", relay_same, 0, 1)
+    scoped("r_s11", relay_same, 1, 1)
     with jax.named_scope("weights"):
         for copy in own_weights:
             copy.wait()
@@ -432,12 +475,11 @@
     scoped("ratio0s", ratio_of, 0, same)
     scoped("r_c10a", relay, 1, 0, first)
     scoped("r_c10b", relay, 1, 0, later)
-    send_cross(0, 1)
-    scoped("r_s11", relay_same, 1, 1)
+    next_cross(1)
     scoped("r_s20", relay_same, 2, 0)
     scoped("r_c20a", relay, 2, 0, first)
     scoped("r_c20b", relay, 2, 0, later)
-    send_cross(1, 1)
+    next_cross(2)
     scoped("w_s20", wait_unit, 2, 0, same)
     scoped("sums0s", sums_of, 0, same)
     scoped("r_c01a", relay, 0, 1, first)
@@ -445,7 +487,7 @@
     scoped("w_c10", wait_unit, 1, 0, cross)
     scoped("ratio0c", ratio_of, 0, cross)
     scoped("r_c01b", relay, 0, 1, later)
-    send_cross(2, 1)
+    next_cross(3)
     scoped("w_c20", wait_unit, 2, 0, cross)
     scoped("sums0c", sums_of, 0, cross)
     scoped("w_s01", wait_unit, 0, 1, same)
@@ -453,16 +495,19 @@
     scoped("ratio1s", ratio_of, 1, same)
     scoped("r_c11a", relay, 1, 1, first)
     scoped("r_c11b", relay, 1, 1, later)
+    next_cross(4)
     scoped("back0s", send_back, 0, same)
     scoped("r_c21a", relay, 2, 1, first)
-    scoped("back0c", send_back, 0, cross)
+    scoped("back0c", send_back, 0, cross, 0, 1)
+    scoped("r_c21b", relay, 2, 1, later)
+    scoped("r_s21", relay_same, 2, 1, range(1, half - 1))
+    scoped("back0c2", send_back, 0, cross, 1)
     scoped("w_c01", wait_unit, 0, 1, cross)
     scoped("w_c11", wait_unit, 1, 1, cross)
     scoped("ratio1c", ratio_of, 1, cross)
-    scoped("r_c21b", relay, 2, 1, later)
-    scoped("r_s21", relay_same, 2, 1)
     scoped("w_c21", wait_unit, 2, 1, cross)
-    scoped("sums1c", sums_of, 1, cross)
+    scoped("sums1c", sums_of, 1, cross, None, functools.partial(relay_same, 2, 1, [half - 1]))
+    scoped("back1c", back_chunk, 1, cross, 0)
     scoped("w_s21", wait_unit, 2, 1, same)
     scoped("sums1s", sums_of, 1, same, functools.partial(back_chunk, 1, cross))
     scoped("back1s", send_back, 1, same)
@@ -473,32 +518,22 @@
     got_row = other * (n_local * half_rows) + in_half
     got_col = column(got_row.astype(f32))
 
-    def pick_of(kind):
-        shape = (tokens, n_local * half_rows)
-        at = lax.broadcasted_iota(jnp.int32, shape, 1) + kind * n_local * half_rows
-        return jnp.where(at.astype(f32) == got_col, 1.0, 0.0).astype(bf16)
+    at = lax.broadcasted_iota(jnp.int32, (tokens, n_local * rows), 1)
+    pick = jnp.where(at.astype(f32) == got_col, 1.0, 0.0).astype(bf16)
 
     def wait_back(kind, c):
         remote = len(steps_of(kind)) * cap
         await_bytes(back.at[kind, :, pl.ds(0, remote), chunk_of(c)], back_recv.at[kind, c])
 
-    def got_of(kind, cols):
-        return back[kind, :, :, cols].reshape(n_local * half_rows, chunk)
-
-    with jax.named_scope("pick_c"):
-        pick = pick_of(cross)
-        for c in range(n_chunks):
-            wait_back(cross, c)
-            cols = chunk_of(c)
-            layer[:, cols] += scale[:, cols] * jnp.dot(pick, got_of(cross, cols), preferred_element_type=f32)
-    with jax.named_scope("pick_s"):
-        pick = pick_of(same)
-        for c in range(n_chunks):
-            cols = chunk_of(c)
-            with jax.named_scope(f"w_{c}"):
-                wait_back(same, c)
+    for c in range(n_chunks):
+        cols = chunk_of(c)
+        for kind in (cross, same):
+            with jax.named_scope(f"w_{kind}{c}"):
+                wait_back(kind, c)
+        got = back[:, :, :, cols].reshape(n_local * rows, chunk)
+        with jax.named_scope(f"pick{c}"):
             out[:, cols] = (
-                layer[:, cols] + scale[:, cols] * jnp.dot(pick, got_of(same, cols), preferred_element_type=f32)
+                layer[:, cols] + scale[:, cols] * jnp.dot(pick, got, preferred_element_type=f32)
             ).astype(bf16)
 
     with jax.named_scope("drain"):
@@ -562,11 +597,11 @@
             dma((2,)),
             dma((2,)),
             dma((1,)),
-            dma((3, n_local, n_peers)),
+            dma((3 * n_local * (n_peers // 2 + 1) + n_peers // 2 - 2,)),
             dma((1,)),
             dma((3, n_local, 2)),
             dma((1,)),
-            dma((n_local, 2, n_chunks)),
+            dma((2 + 2 * n_chunks,)),
             dma((1,)),
             dma((2, n_chunks)),
         ],

time: 105 us -> 104 us (level)
  no operation moved by 1% of the time
where the time goes in v3:
time: 104 us; the launch traced here: 103 us
  Pallas kernels  102 us (98%)
    pallas_call x1, Pallas kernels, whole_pass(): pl.pallas_call(functools.partial(whole_kernel, n_peers, n_dp, cap, chunk)...  102 us

profile of v3, /device:TPU:0, one launch (start us, length us, event | category | flops | bytes accessed | tf_op | source)
XLA Modules:
  0.0 103.4 jit_solution(16338091516167757350)
XLA Ops:
  0.7 101.9 %whole_pass.1 = bf16[256,1024]{1,0:T(8,128)(2,1)S(1)} custom-call(bf16[256,1024]{1,0:T(8,128)(2,1)} %bitcast.15, bf16[256,1024]{1,0:T(8,128)(2,1)} %bitcast.16, s32[1,256]{1,0:T(1,128)} %bitcast.21, s32[1,256]{1,0:T(1,128)} %bitcast.22, f32[1,256]{1,0:T(1,128)} %bitcast.23, f32[1,1024]{1,0:T(1,128)} %bitcast.20, s32[1,1]{1,0:T(1,128)S(6)} %copy.16.length_at, ...), custom_call_target="tpu_custom_call" | custom-call | tf_op jit(solution)/shard_map/whole_pass/pallas_call | solution.py:564
  102.6 0.8 copy.15

commit v4 on v3

--- a/solution.py
+++ b/solution.py
@@ -147,6 +147,13 @@
     def load(pairs, first_sem):
         copies = []
         for at, (ref, held_at) in enumerate(pairs):
+            if at + first_sem == 0:
+                quarter = tokens // 4
+                for part in range(4):
+                    some = pl.ds(part * quarter, quarter)
+                    pltpu.make_async_copy(ref.at[some], held_at.at[some], load_sem.at[0]).start()
+                copies.append(pltpu.make_async_copy(ref, held_at, load_sem.at[0]))
+                continue
             copy = pltpu.make_async_copy(ref, held_at, load_sem.at[first_sem + at])
             copy.start()
             copies.append(copy)
@@ -296,15 +303,8 @@
     send_same(1, 0)
     place_rows(0, 1, inputs)
     own_hop(0, 1).start()
-    send_same(0, 1)
-
-    @pl.when(inner == 1)
-    def _():
-        send_cross(1, 0)
-
     place_rows(1, 1, base_inputs)
     own_hop(1, 1).start()
-    send_same(1, 1)
     for l in range(n_local):
         for a in range(2):
             keep_own(a, l)
@@ -346,11 +346,17 @@
 
     pieces = width // (2 * HEAD_DIM)
     with jax.named_scope("attn0"):
-        pl.loop(0, pieces - 1)(two_heads)
+        pl.loop(0, pieces - 2)(two_heads)
     with jax.named_scope("r_s00"):
         relay(0, 0, range(1, half - 1))
+    send_same(0, 1)
+
+    @pl.when(inner == 1)
+    def _():
+        send_cross(1, 0)
+
     with jax.named_scope("attn1"):
-        pl.loop(pieces - 1, pieces)(two_heads)
+        pl.loop(pieces - 2, pieces)(two_heads)
 
     def chunk_of(c):
         return pl.ds(pl.multiple_of(c * chunk, chunk), chunk)
@@ -363,8 +369,7 @@
 
     with jax.named_scope("r_c00a"):
         relay(0, 0, first[:1])
-    with jax.named_scope("r_s00b"):
-        relay(0, 0, [half - 1])
+    send_same(1, 1)
     scaled = (column(gate[...]) * layer[...]).astype(bf16)
     for l in range(n_local):
         place_rows(2, l, scaled)
@@ -459,6 +464,7 @@
         with jax.named_scope(name):
             call(*args)
 
+    scoped("r_s00b", relay, 0, 0, [half - 1])
     scoped("r_c00b", relay, 0, 0, first[1:])
     scoped("r_c00c", relay, 0, 0, later)
     next_cross(0)

time: 104 us -> 103 us (level)
  no operation moved by 1% of the time
where the time goes in v4:
time: 103 us
  Pallas kernels  102 us (99%)
    pallas_call x1, Pallas kernels, whole_pass(): pl.pallas_call(functools.partial(whole_kernel, n_peers, n_dp, cap, chunk)...  102 us

profile of v4, /device:TPU:0, one launch (start us, length us, event | category | flops | bytes accessed | tf_op | source)
XLA Modules:
  0.0 103.1 jit_solution(6075850307042331863)
XLA Ops:
  0.7 101.6 %whole_pass.1 = bf16[256,1024]{1,0:T(8,128)(2,1)S(1)} custom-call(bf16[256,1024]{1,0:T(8,128)(2,1)} %bitcast.15, bf16[256,1024]{1,0:T(8,128)(2,1)} %bitcast.16, s32[1,256]{1,0:T(1,128)} %bitcast.21, s32[1,256]{1,0:T(1,128)} %bitcast.22, f32[1,256]{1,0:T(1,128)} %bitcast.23, f32[1,1024]{1,0:T(1,128)} %bitcast.20, s32[1,1]{1,0:T(1,128)S(6)} %copy.16.length_at, ...), custom_call_target="tpu_custom_call" | custom-call | tf_op jit(solution)/shard_map/whole_pass/pallas_call | solution.py:570
  102.3 0.8 copy.15

commit v5 on v4

--- a/solution.py
+++ b/solution.py
@@ -504,10 +504,18 @@
     next_cross(4)
     scoped("back0s", send_back, 0, same)
     scoped("r_c21a", relay, 2, 1, first)
-    scoped("back0c", send_back, 0, cross, 0, 1)
+
+    @pl.when(inner == 1)
+    def _():
+        scoped("back0c", send_back, 0, cross, 0, 4)
+
     scoped("r_c21b", relay, 2, 1, later)
     scoped("r_s21", relay_same, 2, 1, range(1, half - 1))
-    scoped("back0c2", send_back, 0, cross, 1)
+
+    @pl.when(inner == 0)
+    def _():
+        scoped("back0c2", send_back, 0, cross)
+
     scoped("w_c01", wait_unit, 0, 1, cross)
     scoped("w_c11", wait_unit, 1, 1, cross)
     scoped("ratio1c", ratio_of, 1, cross)

time: 103 us -> 103 us (level)
  no operation moved by 1% of the time
where the time goes in v5:
time: 103 us
  Pallas kernels  102 us (99%)
    pallas_call x1, Pallas kernels, whole_pass(): pl.pallas_call(functools.partial(whole_kernel, n_peers, n_dp, cap, chunk)...  102 us

profile of v5, /device:TPU:0, one launch (start us, length us, event | category | flops | bytes accessed | tf_op | source)
XLA Modules:
  0.0 103.1 jit_solution(5552076225234612254)
XLA Ops:
  0.7 101.6 %whole_pass.1 = bf16[256,1024]{1,0:T(8,128)(2,1)S(1)} custom-call(bf16[256,1024]{1,0:T(8,128)(2,1)} %bitcast.15, bf16[256,1024]{1,0:T(8,128)(2,1)} %bitcast.16, s32[1,256]{1,0:T(1,128)} %bitcast.21, s32[1,256]{1,0:T(1,128)} %bitcast.22, f32[1,256]{1,0:T(1,128)} %bitcast.23, f32[1,1024]{1,0:T(1,128)} %bitcast.20, s32[1,1]{1,0:T(1,128)S(6)} %copy.16.length_at, ...), custom_call_target="tpu_custom_call" | custom-call | tf_op jit(solution)/shard_map/whole_pass/pallas_call | solution.py:578
  102.3 0.8 copy.15

commit v6 on v5

--- a/solution.py
+++ b/solution.py
@@ -206,8 +206,8 @@
     def arrival_of(a, l, step):
         at = a + 3 * l
         if step >= half:
-            return at * half + step - half
-        apart = 3 * n_local * half
+            return at * 2 + (half - 2 + step % 2 if at else step - half)
+        apart = 3 * n_local * 2 + half - 2
         return apart + at if at or step == 1 else apart + 3 * n_local + step - 2
 
     def row_copy(a, l, step):
@@ -231,7 +231,7 @@
             src_ref=held.at[a, l, kind, near_block(src), :],
             dst_ref=held.at[a, l, kind, far_block(src), :],
             send_sem=hop_send.at[0],
-            recv_sem=hop_recv.at[a, l, kind],
+            recv_sem=hop_recv.at[a // 2, l, kind],
             device_id={"dp": across},
             device_id_type=mesh_id,
         )
@@ -241,7 +241,7 @@
             src_ref=sends.at[a, l, block_of(me), :],
             dst_ref=held.at[a, l, same, far_block(me), :],
             send_sem=hop_send.at[0],
-            recv_sem=hop_recv.at[a, l, same],
+            recv_sem=hop_recv.at[a // 2, l, same],
             device_id={"dp": across},
             device_id_type=mesh_id,
         )
@@ -277,13 +277,20 @@
             hop_copy(a, l, same, step).start()
 
     def relay(a, l, steps):
+        if a + 3 * l:
+            size = len(steps) * cap
+            await_bytes(held.at[a, l, cross, pl.ds(0, size), :], row_recv.at[arrival_of(a, l, steps[0])])
+            for step in steps:
+                hop_copy(a, l, cross, step).start()
+            return
         for step in steps:
             kind = step // half
             await_bytes(held.at[a, l, kind, pl.ds(0, cap), :], row_recv.at[arrival_of(a, l, step)])
             hop_copy(a, l, kind, step).start()
 
     def wait_unit(a, l, kind):
-        await_bytes(held.at[a, l, kind, pl.ds(half_rows, half_rows), :], hop_recv.at[a, l, kind])
+        arrays = pl.ds(0, 2) if a < 2 else pl.ds(2, 1)
+        await_bytes(held.at[arrays, l, kind, pl.ds(half_rows, half_rows), :], hop_recv.at[a // 2, l, kind])
 
     token_rows = state[...].astype(f32)
     scale[...] = gain[...] * lax.rsqrt(
@@ -476,7 +483,6 @@
             copy.wait()
         for swap in swaps:
             swap.wait_recv()
-    scoped("w_s00", wait_unit, 0, 0, same)
     scoped("w_s10", wait_unit, 1, 0, same)
     scoped("ratio0s", ratio_of, 0, same)
     scoped("r_c10a", relay, 1, 0, first)
@@ -489,14 +495,12 @@
     scoped("w_s20", wait_unit, 2, 0, same)
     scoped("sums0s", sums_of, 0, same)
     scoped("r_c01a", relay, 0, 1, first)
-    scoped("w_c00", wait_unit, 0, 0, cross)
     scoped("w_c10", wait_unit, 1, 0, cross)
     scoped("ratio0c", ratio_of, 0, cross)
     scoped("r_c01b", relay, 0, 1, later)
     next_cross(3)
     scoped("w_c20", wait_unit, 2, 0, cross)
     scoped("sums0c", sums_of, 0, cross)
-    scoped("w_s01", wait_unit, 0, 1, same)
     scoped("w_s11", wait_unit, 1, 1, same)
     scoped("ratio1s", ratio_of, 1, same)
     scoped("r_c11a", relay, 1, 1, first)
@@ -516,7 +520,6 @@
     def _():
         scoped("back0c2", send_back, 0, cross)
 
-    scoped("w_c01", wait_unit, 0, 1, cross)
     scoped("w_c11", wait_unit, 1, 1, cross)
     scoped("ratio1c", ratio_of, 1, cross)
     scoped("w_c21", wait_unit, 2, 1, cross)
@@ -611,9 +614,9 @@
             dma((2,)),
             dma((2,)),
             dma((1,)),
-            dma((3 * n_local * (n_peers // 2 + 1) + n_peers // 2 - 2,)),
+            dma((3 * n_local * 3 + 2 * (n_peers // 2 - 2),)),
             dma((1,)),
-            dma((3, n_local, 2)),
+            dma((2, n_local, 2)),
             dma((1,)),
             dma((2 + 2 * n_chunks,)),
             dma((1,)),

time: 103 us -> 103 us (level)
  no operation moved by 1% of the time
where the time goes in v6:
time: 103 us
  Pallas kernels  101 us (98%)
    pallas_call x1, Pallas kernels, whole_pass(): pl.pallas_call(functools.partial(whole_kernel, n_peers, n_dp, cap, chunk)...  101 us

profile of v6, /device:TPU:0, one launch (start us, length us, event | category | flops | bytes accessed | tf_op | source)
XLA Modules:
  0.0 103.0 jit_solution(15111740909875453179)
XLA Ops:
  0.7 101.5 %whole_pass.1 = bf16[256,1024]{1,0:T(8,128)(2,1)S(1)} custom-call(bf16[256,1024]{1,0:T(8,128)(2,1)} %bitcast.15, bf16[256,1024]{1,0:T(8,128)(2,1)} %bitcast.16, s32[1,256]{1,0:T(1,128)} %bitcast.21, s32[1,256]{1,0:T(1,128)} %bitcast.22, f32[1,256]{1,0:T(1,128)} %bitcast.23, f32[1,1024]{1,0:T(1,128)} %bitcast.20, s32[1,1]{1,0:T(1,128)S(6)} %copy.16.length_at, ...), custom_call_target="tpu_custom_call" | custom-call | tf_op jit(solution)/shard_map/whole_pass/pallas_call | solution.py:581
  102.2 0.8 copy.15

commit v7 on v6

--- a/solution.py
+++ b/solution.py
@@ -353,7 +353,7 @@
 
     pieces = width // (2 * HEAD_DIM)
     with jax.named_scope("attn0"):
-        pl.loop(0, pieces - 2)(two_heads)
+        pl.loop(0, pieces - 3)(two_heads)
     with jax.named_scope("r_s00"):
         relay(0, 0, range(1, half - 1))
     send_same(0, 1)
@@ -363,7 +363,7 @@
         send_cross(1, 0)
 
     with jax.named_scope("attn1"):
-        pl.loop(pieces - 2, pieces)(two_heads)
+        pl.loop(pieces - 3, pieces)(two_heads)
 
     def chunk_of(c):
         return pl.ds(pl.multiple_of(c * chunk, chunk), chunk)

time: 103 us -> 103 us (level)
  no operation moved by 1% of the time
where the time goes in v7:
time: 103 us
  Pallas kernels  101 us (98%)
    pallas_call x1, Pallas kernels, whole_pass(): pl.pallas_call(functools.partial(whole_kernel, n_peers, n_dp, cap, chunk)...  101 us

profile of v7, /device:TPU:0, one launch (start us, length us, event | category | flops | bytes accessed | tf_op | source)
XLA Modules:
  0.0 103.0 jit_solution(18315917508576380786)
XLA Ops:
  0.7 101.5 %whole_pass.1 = bf16[256,1024]{1,0:T(8,128)(2,1)S(1)} custom-call(bf16[256,1024]{1,0:T(8,128)(2,1)} %bitcast.15, bf16[256,1024]{1,0:T(8,128)(2,1)} %bitcast.16, s32[1,256]{1,0:T(1,128)} %bitcast.21, s32[1,256]{1,0:T(1,128)} %bitcast.22, f32[1,256]{1,0:T(1,128)} %bitcast.23, f32[1,1024]{1,0:T(1,128)} %bitcast.20, s32[1,1]{1,0:T(1,128)S(6)} %copy.16.length_at, ...), custom_call_target="tpu_custom_call" | custom-call | tf_op jit(solution)/shard_map/whole_pass/pallas_call | solution.py:581
  102.2 0.8 copy.15
